TPU v7x, 512 devices: a whole 4x8x8 slice. The times are simulated.
512 devices in a mesh: dp: 8 (over x, core), ctx: 64 (over y, z).
Axes of the slice: x: 4, y: 8, z: 8, core: 2. Of those that a mesh axis runs over, the one named last changes fastest.
Arguments:
- queries: bfloat16 [16, 4096, 2048], P('dp', 'ctx'), may hold values from -52 to 52
- key_rows: bfloat16 [16, 4096, 2048], P('dp', 'ctx'), may hold values from -4 to 4
- value_rows: bfloat16 [16, 4096, 2048], P('dp', 'ctx'), may hold values from -6 to 6
- out_grad: bfloat16 [16, 4096, 2048], P('dp', 'ctx'), may hold values from -64 to 64
- level_slope: float32 [16], replicated, may hold values from -0.5 to 0.5
Outputs:
- query_grad: bfloat16 [16, 4096, 2048], P('dp', 'ctx')
- key_grad: bfloat16 [16, 4096, 2048], P('dp', 'ctx')
- value_grad: bfloat16 [16, 4096, 2048], P('dp', 'ctx')
- slope_grad: float32 [16], replicated
All inputs are finite; a program needn't handle non-finite values.
Results may differ from a plain program's by a relative error of at most 0.0075.
Values may be sent and summed in bfloat16 or wider, within the bound.
A program may use at most 64 MiB of HBM per device.

v0:
```python
import math
import jax
import jax.numpy as jnp
from jax import lax
from jax.sharding import PartitionSpec as P


def as_sent(x):
    return jax.tree.map(lambda a: a.astype(jnp.bfloat16) if a.dtype == jnp.float32 else a, x)


def from_partner(value, axis, apart):
    mask = 2**apart
    pairs = [(source, source ^ mask) for source in range(lax.axis_size(axis))]
    return lax.ppermute(value, axis, pairs)


def pair_mean(cells):
    shaped = cells.reshape(cells.shape[:-2] + (cells.shape[-2] // 2, 2, cells.shape[-1])).astype(
        jnp.float32
    )
    return ((shaped[..., 0, :] + shaped[..., 1, :]) * 0.5).astype(jnp.bfloat16)


def merge_level(own_pair, other_pair, flag):
    merged = []
    for own_part, other_part in zip(own_pair, other_pair):
        own_small = pair_mean(own_part)
        other_small = pair_mean(other_part)
        merged.append(
            jnp.where(
                flag == 1,
                jnp.concatenate([other_small, own_small], axis=1),
                jnp.concatenate([own_small, other_small], axis=1),
            )
        )
    return tuple(merged)


def to_heads(rows, heads):
    seqs, count, width = rows.shape
    return jnp.transpose(rows.reshape(seqs, count, heads, width // heads), (0, 2, 1, 3))


def from_heads(split):
    seqs, heads, count, head = split.shape
    return jnp.transpose(split, (0, 2, 1, 3)).reshape(seqs, count, heads * head)


def product(form, left, right):
    return jnp.einsum(form, left, right, preferred_element_type=jnp.float32)


def attend(query_four, key_four, value_four, grad_four, level_slope, block):
    head = query_four.shape[3]
    key_count = key_four.shape[2]
    scale = 1.0 / math.sqrt(head)
    column = jnp.arange(key_count, dtype=jnp.int32)
    level_of = column // block - 1
    sibling = jnp.maximum(level_of, 0)
    multiple = jnp.where(level_of < 0, 1.0, jnp.exp2(sibling.astype(jnp.float32)))
    bias = level_slope[:, None] * sibling.astype(jnp.float32)[None, :]
    raw = product("shqd,shkd->shqk", query_four, key_four)
    scores = raw * scale + bias[None, :, None, :]
    top = jnp.max(scores, axis=-1, keepdims=True)
    weights = multiple[None, None, None, :] * jnp.exp(scores - top)
    probs = weights / jnp.sum(weights, axis=-1, keepdims=True)
    probs_low = probs.astype(jnp.bfloat16)
    output = product("shqk,shkd->shqd", probs_low, value_four)
    delta = jnp.sum(grad_four.astype(jnp.float32) * output, axis=-1)
    upstream = product("shqd,shkd->shqk", grad_four, value_four)
    dscore = probs * (upstream - delta[..., None])
    slope_part = jnp.sum(dscore * sibling.astype(jnp.float32)[None, None, None, :], axis=(0, 2, 3))
    dscore_low = dscore.astype(jnp.bfloat16)
    query_part = product("shqk,shkd->shqd", dscore_low, key_four) * scale
    key_part = product("shqk,shqd->shkd", dscore_low, query_four) * scale
    value_part = product("shqk,shqd->shkd", probs_low, grad_four)
    return (query_part, key_part, value_part, slope_part)


def split_level(grad_now, direct, flag, level, block):
    half = block // 2
    lower_src = grad_now[:, :, :half]
    upper_src = grad_now[:, :, half:]
    own_src = jnp.where(flag == 1, upper_src, lower_src)
    other_src = jnp.where(flag == 1, lower_src, upper_src)
    own_half = jnp.repeat(own_src, 2, axis=2) * 0.5
    other_half = jnp.repeat(other_src, 2, axis=2) * 0.5
    sent = (other_half + direct[:, :, (level + 1) * block : (level + 2) * block]).astype(
        jnp.bfloat16
    )
    return (own_half, sent)


def shards(queries, key_rows, value_rows, out_grad, level_slope):
    seqs, block, width = queries.shape
    heads = level_slope.shape[0]
    ctx_count = lax.axis_size("ctx")
    levels = ctx_count.bit_length() - 1
    position = lax.axis_index("ctx")
    bit_list = [position // 2**level % 2 for level in range(levels)]
    own_pair = (key_rows, value_rows)
    partners = []
    for level in range(levels - 2):
        other_pair = jax.tree.map(
            lambda part, own: part.astype(own.dtype),
            from_partner(as_sent(own_pair), "ctx", level),
            own_pair,
        )
        partners.append(other_pair)
        own_pair = merge_level(own_pair, other_pair, bit_list[level])
    for level in range(levels - 2, levels):
        other_pair = jax.tree.map(
            lambda part, own: part.astype(own.dtype),
            from_partner(as_sent(own_pair), "ctx", level),
            own_pair,
        )
        partners.append(other_pair)
        if level + 1 < levels:
            own_pair = merge_level(own_pair, other_pair, bit_list[level])
    key_set = jnp.concatenate(
        [to_heads(key_rows, heads)] + [to_heads(pair[0], heads) for pair in partners], axis=2
    )
    value_set = jnp.concatenate(
        [to_heads(value_rows, heads)] + [to_heads(pair[1], heads) for pair in partners], axis=2
    )
    query_four = to_heads(queries, heads)
    grad_four = to_heads(out_grad, heads)
    query_part, key_part, value_part, slope_part = attend(
        query_four, key_set, value_set, grad_four, level_slope, block
    )
    slope_grad = lax.psum(slope_part, ("dp", "ctx"))
    head = width // heads
    grad_keys = jnp.zeros((seqs, heads, block, head), jnp.float32)
    grad_values = jnp.zeros((seqs, heads, block, head), jnp.float32)
    for level in reversed(range(levels)):
        own_keys, sent_keys = split_level(grad_keys, key_part, bit_list[level], level, block)
        own_values, sent_values = split_level(
            grad_values, value_part, bit_list[level], level, block
        )
        back_keys, back_values = from_partner((sent_keys, sent_values), "ctx", level)
        grad_keys = own_keys + back_keys.astype(jnp.float32)
        grad_values = own_values + back_values.astype(jnp.float32)
    key_grad = from_heads((grad_keys + key_part[:, :, :block]).astype(jnp.bfloat16))
    value_grad = from_heads((grad_values + value_part[:, :, :block]).astype(jnp.bfloat16))
    return (from_heads(query_part.astype(jnp.bfloat16)), key_grad, value_grad, slope_grad)


def solution(mesh):
    placed = (
        P("dp", "ctx", None),
        P("dp", "ctx", None),
        P("dp", "ctx", None),
        P("dp", "ctx", None),
        P(),
    )
    return jax.shard_map(
        shards,
        mesh=mesh,
        in_specs=placed,
        out_specs=(P("dp", "ctx", None), P("dp", "ctx", None), P("dp", "ctx", None), P()),
        check_vma=False,
    )
```

profile of v0, /device:TPU:1, one launch (start us, length us, event | category | flops | bytes accessed | tf_op | source)
XLA Modules:
  0.0 589.4 jit_solution(14422107451718763266)
XLA Ops:
  0.7 5.0 collective-permute-start
  10.9 2.0 fusion.33
  15.2 9.6 %collective-permute-done.6 = bf16[2,64,2048]{2,1,0:T(8,128)(2,1)} collective-permute-done((bf16[2,64,2048]{2,1,0:T(8,128)(2,1)}, bf16[2,64,2048]{2,1,0:T(8,128)(2,1)}, u32[]{:S(2)}, u32[]{:S(2)}) %collective-permute-start.6) | collective-permute-done | bytes 524320 | tf_op jit(solution)/shard_map/ppermute | solution.py:15
  30.0 9.8 %collective-permute-start.1 = (bf16[2,64,2048]{2,0,1:T(2,128)(2,1)S(1)}, bf16[2,64,2048]{2,0,1:T(2,128)(2,1)S(1)}, u32[]{:S(2)}, u32[]{:S(2)}) collective-permute-start(bf16[2,64,2048]{2,0,1:T(2,128)(2,1)S(1)} %broadcast_select_fusion.9), channel_id=1, source_target_pairs={{0,2},{1,3},{2,0},{3,1},{4,6},{5,7},{6,4},{7,5},{8,10},{9,11},{10,... | collective-permute-start | bytes 1572872 | tf_op jit(solution)/shard_map/ppermute | solution.py:15
  44.0 2.0 fusion.32
  46.0 2.0 fusion.29
  48.0 25.8 %collective-permute-done.1 = bf16[2,64,2048]{2,0,1:T(2,128)(2,1)S(1)} collective-permute-done((bf16[2,64,2048]{2,0,1:T(2,128)(2,1)S(1)}, bf16[2,64,2048]{2,0,1:T(2,128)(2,1)S(1)}, u32[]{:S(2)}, u32[]{:S(2)}) %collective-permute-start.1) | collective-permute-done | bytes 524320 | tf_op jit(solution)/shard_map/ppermute | solution.py:15
  76.5 8.4 %collective-permute-start.2 = (bf16[2,64,2048]{2,0,1:T(2,128)(2,1)S(1)}, bf16[2,64,2048]{2,0,1:T(2,128)(2,1)S(1)}, u32[]{:S(2)}, u32[]{:S(2)}) collective-permute-start(bf16[2,64,2048]{2,0,1:T(2,128)(2,1)S(1)} %broadcast_select_fusion.7), channel_id=1, source_target_pairs={{0,4},{1,5},{2,6},{3,7},{4,0},{5,1},{6,2},{7,3},{8,12},{9,13},{10,... | collective-permute-start | bytes 1572872 | tf_op jit(solution)/shard_map/ppermute | solution.py:15
  87.3 1.9 broadcast_select_fusion.6
  89.3 30.1 %collective-permute-start.8 = (bf16[2,64,2048]{2,0,1:T(2,128)(2,1)}, bf16[2,64,2048]{2,0,1:T(2,128)(2,1)S(1)}, u32[]{:S(2)}, u32[]{:S(2)}) collective-permute-start(bf16[2,64,2048]{2,0,1:T(2,128)(2,1)} %broadcast_select_fusion.6), channel_id=1, source_target_pairs={{0,4},{1,5},{2,6},{3,7},{4,0},{5,1},{6,2},{7,3},{8,12},{9,13},{10,... | collective-permute-start | bytes 1572872 | tf_op jit(solution)/shard_map/ppermute | solution.py:15
  120.5 2.1 bitcast_dynamic-update-slice_fusion.9
  128.0 3.2 collective-permute-start.3
  132.2 9.6 %collective-permute-done.8 = bf16[2,64,2048]{2,0,1:T(2,128)(2,1)S(1)} collective-permute-done((bf16[2,64,2048]{2,0,1:T(2,128)(2,1)}, bf16[2,64,2048]{2,0,1:T(2,128)(2,1)S(1)}, u32[]{:S(2)}, u32[]{:S(2)}) %collective-permute-start.8) | collective-permute-done | bytes 524320 | tf_op jit(solution)/shard_map/ppermute | solution.py:15
  142.8 1.9 broadcast_select_fusion.4
  144.7 3.6 collective-permute-start.9
  149.4 2.1 bitcast_dynamic-update-slice_fusion.8
  157.1 4.2 collective-permute-start.4
  163.2 1.9 broadcast_select_fusion.2
  165.2 2.0 collective-permute-start.10
  168.3 2.1 bitcast_dynamic-update-slice_fusion.7
  173.7 22.1 %collective-permute-done.4 = bf16[2,64,2048]{2,0,1:T(2,128)(2,1)S(1)} collective-permute-done((bf16[2,64,2048]{2,0,1:T(2,128)(2,1)S(1)}, bf16[2,64,2048]{2,0,1:T(2,128)(2,1)S(1)}, u32[]{:S(2)}, u32[]{:S(2)}) %collective-permute-start.4) | collective-permute-done | bytes 524320 | tf_op jit(solution)/shard_map/ppermute | solution.py:15
  196.8 1.9 broadcast_select_fusion.1
  198.8 6.3 %collective-permute-start.5 = (bf16[2,64,2048]{2,0,1:T(2,128)(2,1)}, bf16[2,64,2048]{2,0,1:T(2,128)(2,1)S(1)}, u32[]{:S(2)}, u32[]{:S(2)}) collective-permute-start(bf16[2,64,2048]{2,0,1:T(2,128)(2,1)} %broadcast_select_fusion.1), channel_id=1, source_target_pairs={{0,32},{1,33},{2,34},{3,35},{4,36},{5,37},{6,38},{7,39},{8,40},{9,... | collective-permute-start | bytes 1572872 | tf_op jit(solution)/shard_map/ppermute | solution.py:15
  205.0 2.2 collective-permute-done.10
  208.1 1.9 broadcast_select_fusion
  210.1 20.2 %collective-permute-start.11 = (bf16[2,64,2048]{2,0,1:T(2,128)(2,1)}, bf16[2,64,2048]{2,0,1:T(2,128)(2,1)S(1)}, u32[]{:S(2)}, u32[]{:S(2)}) collective-permute-start(bf16[2,64,2048]{2,0,1:T(2,128)(2,1)} %broadcast_select_fusion), channel_id=1, source_target_pairs={{0,32},{1,33},{2,34},{3,35},{4,36},{5,37},{6,38},{7,39},{8,40},{9,... | collective-permute-start | bytes 1572872 | tf_op jit(solution)/shard_map/ppermute | solution.py:15
  234.4 22.0 %collective-permute-done.11 = bf16[2,64,2048]{2,0,1:T(2,128)(2,1)S(1)} collective-permute-done((bf16[2,64,2048]{2,0,1:T(2,128)(2,1)}, bf16[2,64,2048]{2,0,1:T(2,128)(2,1)S(1)}, u32[]{:S(2)}, u32[]{:S(2)}) %collective-permute-start.11) | collective-permute-done | bytes 524320 | tf_op jit(solution)/shard_map/ppermute | solution.py:15
  257.7 3.7 fusion.31
  266.1 2.1 multiply_reduce_fusion
  269.1 5.7 collective-permute-start.18
  275.7 101.6 %psum.7 = f32[16]{0:T(128)} all-reduce(f32[16]{0:T(128)S(1)} %get-tuple-element.26), channel_id=1, replica_groups=mesh['dp'=8,'ctx'=64] {'dp','ctx'}, use_global_device_ids=true, to_apply=%region_4.5 | all-reduce | flops 16 | bytes 128 | tf_op jit(solution)/shard_map/psum | solution.py:132
  379.5 5.8 collective-permute-start.12
  389.1 20.6 %collective-permute-done.12 = bf16[2,16,64,128]{3,2,1,0:T(8,128)(2,1)S(1)} collective-permute-done((bf16[2,16,64,128]{3,2,1,0:T(8,128)(2,1)S(1)}, bf16[2,16,64,128]{3,2,1,0:T(8,128)(2,1)S(1)}, u32[]{:S(2)}, u32[]{:S(2)}) %collective-permute-start.12) | collective-permute-done | bytes 524320 | tf_op jit(solution)/shard_map/ppermute | solution.py:15
  412.4 30.1 %collective-permute-done.19 = bf16[2,16,64,128]{3,2,1,0:T(8,128)(2,1)S(1)} collective-permute-done((bf16[2,16,64,128]{3,2,1,0:T(8,128)(2,1)S(1)}, bf16[2,16,64,128]{3,2,1,0:T(8,128)(2,1)S(1)}, u32[]{:S(2)}, u32[]{:S(2)}) %collective-permute-start.19) | collective-permute-done | bytes 524320 | tf_op jit(solution)/shard_map/ppermute | solution.py:15
  443.8 2.4 collective-permute-start.20
  446.3 7.6 %collective-permute-done.13 = bf16[2,16,64,128]{3,2,1,0:T(8,128)(2,1)S(1)} collective-permute-done((bf16[2,16,64,128]{3,2,1,0:T(8,128)(2,1)S(1)}, bf16[2,16,64,128]{3,2,1,0:T(8,128)(2,1)S(1)}, u32[]{:S(2)}, u32[]{:S(2)}) %collective-permute-start.13) | collective-permute-done | bytes 524320 | tf_op jit(solution)/shard_map/ppermute | solution.py:15
  455.0 2.4 collective-permute-start.14
  457.5 7.5 %collective-permute-done.20 = bf16[2,16,64,128]{3,2,1,0:T(8,128)(2,1)S(1)} collective-permute-done((bf16[2,16,64,128]{3,2,1,0:T(8,128)(2,1)S(1)}, bf16[2,16,64,128]{3,2,1,0:T(8,128)(2,1)S(1)}, u32[]{:S(2)}, u32[]{:S(2)}) %collective-permute-start.20) | collective-permute-done | bytes 524320 | tf_op jit(solution)/shard_map/ppermute | solution.py:15
  466.3 5.2 collective-permute-start.21
  471.5 4.7 collective-permute-done.14
  477.5 5.2 collective-permute-start.15
  482.7 24.9 %collective-permute-done.21 = bf16[2,16,64,128]{3,2,1,0:T(8,128)(2,1)S(1)} collective-permute-done((bf16[2,16,64,128]{3,2,1,0:T(8,128)(2,1)S(1)}, bf16[2,16,64,128]{3,2,1,0:T(8,128)(2,1)S(1)}, u32[]{:S(2)}, u32[]{:S(2)}) %collective-permute-start.21) | collective-permute-done | bytes 524320 | tf_op jit(solution)/shard_map/ppermute | solution.py:15
  510.8 8.1 %collective-permute-done.15 = bf16[2,16,64,128]{3,2,1,0:T(8,128)(2,1)S(1)} collective-permute-done((bf16[2,16,64,128]{3,2,1,0:T(8,128)(2,1)S(1)}, bf16[2,16,64,128]{3,2,1,0:T(8,128)(2,1)S(1)}, u32[]{:S(2)}, u32[]{:S(2)}) %collective-permute-start.15) | collective-permute-done | bytes 524320 | tf_op jit(solution)/shard_map/ppermute | solution.py:15
  520.2 2.2 collective-permute-start.16
  522.4 31.5 %collective-permute-done.22 = bf16[2,16,64,128]{3,2,1,0:T(8,128)(2,1)S(1)} collective-permute-done((bf16[2,16,64,128]{3,2,1,0:T(8,128)(2,1)S(1)}, bf16[2,16,64,128]{3,2,1,0:T(8,128)(2,1)S(1)}, u32[]{:S(2)}, u32[]{:S(2)}) %collective-permute-start.22) | collective-permute-done | bytes 524320 | tf_op jit(solution)/shard_map/ppermute | solution.py:15
  557.0 8.1 %collective-permute-done.16 = bf16[2,16,64,128]{3,2,1,0:T(8,128)(2,1)S(1)} collective-permute-done((bf16[2,16,64,128]{3,2,1,0:T(8,128)(2,1)S(1)}, bf16[2,16,64,128]{3,2,1,0:T(8,128)(2,1)S(1)}, u32[]{:S(2)}, u32[]{:S(2)}) %collective-permute-start.16) | collective-permute-done | bytes 524320 | tf_op jit(solution)/shard_map/ppermute | solution.py:15
  568.3 8.0 %collective-permute-done.23 = bf16[2,16,64,128]{3,2,1,0:T(8,128)(2,1)S(1)} collective-permute-done((bf16[2,16,64,128]{3,2,1,0:T(8,128)(2,1)S(1)}, bf16[2,16,64,128]{3,2,1,0:T(8,128)(2,1)S(1)}, u32[]{:S(2)}, u32[]{:S(2)}) %collective-permute-start.23) | collective-permute-done | bytes 524320 | tf_op jit(solution)/shard_map/ppermute | solution.py:15
  577.7 9.9 %collective-permute-done.17 = bf16[2,16,64,128]{3,2,1,0:T(8,128)(2,1)S(1)} collective-permute-done((bf16[2,16,64,128]{3,2,1,0:T(8,128)(2,1)S(1)}, bf16[2,16,64,128]{3,2,1,0:T(8,128)(2,1)S(1)}, u32[]{:S(2)}, u32[]{:S(2)}) %collective-permute-start.17) | collective-permute-done | bytes 524320 | tf_op jit(solution)/shard_map/ppermute | solution.py:15
  (161 shorter events, 83.7 us)
Async XLA Ops:
  0.6 262.4 %copy-start = (bf16[2,64,2048]{2,1,0:T(8,128)(2,1)S(1)}, bf16[2,64,2048]{2,1,0:T(8,128)(2,1)}, u32[]{:S(2)}) copy-start(bf16[2,64,2048]{2,1,0:T(8,128)(2,1)} %param.8) | copy-start | bytes 1572868
  0.6 12.2 %copy-start.5 = (bf16[2,64,2048]{2,1,0:T(8,128)(2,1)S(1)}, bf16[2,64,2048]{2,1,0:T(8,128)(2,1)}, u32[]{:S(2)}) copy-start(bf16[2,64,2048]{2,1,0:T(8,128)(2,1)} %param.7) | copy-start | bytes 1572868
  0.7 26.2 %collective-permute-start = (bf16[2,64,2048]{2,1,0:T(8,128)(2,1)}, bf16[2,64,2048]{2,1,0:T(8,128)(2,1)}, u32[]{:S(2)}, u32[]{:S(2)}) collective-permute-start(bf16[2,64,2048]{2,1,0:T(8,128)(2,1)} %param.6), channel_id=1, source_target_pairs={{0,1},{1,0},{2,3},{3,2},{4,5},{5,4},{6,7},{7,6},{8,9},{9,8},{10,11... | collective-permute-start | bytes 1572872 | tf_op jit(solution)/shard_map/ppermute | solution.py:15
  5.6 19.1 %collective-permute-start.6 = (bf16[2,64,2048]{2,1,0:T(8,128)(2,1)}, bf16[2,64,2048]{2,1,0:T(8,128)(2,1)}, u32[]{:S(2)}, u32[]{:S(2)}) collective-permute-start(bf16[2,64,2048]{2,1,0:T(8,128)(2,1)} %param.7), channel_id=1, source_target_pairs={{0,1},{1,0},{2,3},{3,2},{4,5},{5,4},{6,7},{7,6},{8,9},{9,8},{10,11... | collective-permute-start | bytes 1572872 | tf_op jit(solution)/shard_map/ppermute | solution.py:15
  7.7 7.0 %copy-start.7 = (f32[16]{0:T(128)S(1)}, f32[16]{0:T(128)}, u32[]{:S(2)}) copy-start(f32[16]{0:T(128)} %param.9) | copy-start | bytes 196
  30.0 43.8 %collective-permute-start.1 = (bf16[2,64,2048]{2,0,1:T(2,128)(2,1)S(1)}, bf16[2,64,2048]{2,0,1:T(2,128)(2,1)S(1)}, u32[]{:S(2)}, u32[]{:S(2)}) collective-permute-start(bf16[2,64,2048]{2,0,1:T(2,128)(2,1)S(1)} %broadcast_select_fusion.9), channel_id=1, source_target_pairs={{0,2},{1,3},{2,0},{3,1},{4,6},{5,7},{6,4},{7,5},{8,10},{9,11},{10,... | collective-permute-start | bytes 1572872 | tf_op jit(solution)/shard_map/ppermute | solution.py:15
  41.5 44.3 %collective-permute-start.7 = (bf16[2,64,2048]{2,0,1:T(2,128)(2,1)S(1)}, bf16[2,64,2048]{2,0,1:T(2,128)(2,1)S(1)}, u32[]{:S(2)}, u32[]{:S(2)}) collective-permute-start(bf16[2,64,2048]{2,0,1:T(2,128)(2,1)S(1)} %broadcast_select_fusion.8), channel_id=1, source_target_pairs={{0,2},{1,3},{2,0},{3,1},{4,6},{5,7},{6,4},{7,5},{8,10},{9,11},{10,... | collective-permute-start | bytes 1572872 | tf_op jit(solution)/shard_map/ppermute | solution.py:15
  76.5 49.4 %collective-permute-start.2 = (bf16[2,64,2048]{2,0,1:T(2,128)(2,1)S(1)}, bf16[2,64,2048]{2,0,1:T(2,128)(2,1)S(1)}, u32[]{:S(2)}, u32[]{:S(2)}) collective-permute-start(bf16[2,64,2048]{2,0,1:T(2,128)(2,1)S(1)} %broadcast_select_fusion.7), channel_id=1, source_target_pairs={{0,4},{1,5},{2,6},{3,7},{4,0},{5,1},{6,2},{7,3},{8,12},{9,13},{10,... | collective-permute-start | bytes 1572872 | tf_op jit(solution)/shard_map/ppermute | solution.py:15
  89.3 52.5 %collective-permute-start.8 = (bf16[2,64,2048]{2,0,1:T(2,128)(2,1)}, bf16[2,64,2048]{2,0,1:T(2,128)(2,1)S(1)}, u32[]{:S(2)}, u32[]{:S(2)}) collective-permute-start(bf16[2,64,2048]{2,0,1:T(2,128)(2,1)} %broadcast_select_fusion.6), channel_id=1, source_target_pairs={{0,4},{1,5},{2,6},{3,7},{4,0},{5,1},{6,2},{7,3},{8,12},{9,13},{10,... | collective-permute-start | bytes 1572872 | tf_op jit(solution)/shard_map/ppermute | solution.py:15
  128.0 26.9 %collective-permute-start.3 = (bf16[2,64,2048]{2,0,1:T(2,128)(2,1)S(1)}, bf16[2,64,2048]{2,0,1:T(2,128)(2,1)S(1)}, u32[]{:S(2)}, u32[]{:S(2)}) collective-permute-start(bf16[2,64,2048]{2,0,1:T(2,128)(2,1)S(1)} %broadcast_select_fusion.5), channel_id=1, source_target_pairs={{0,8},{1,9},{2,10},{3,11},{4,12},{5,13},{6,14},{7,15},{8,0},{9,1},... | collective-permute-start | bytes 1572872 | tf_op jit(solution)/shard_map/ppermute | solution.py:15
  144.7 17.5 %collective-permute-start.9 = (bf16[2,64,2048]{2,0,1:T(2,128)(2,1)}, bf16[2,64,2048]{2,0,1:T(2,128)(2,1)S(1)}, u32[]{:S(2)}, u32[]{:S(2)}) collective-permute-start(bf16[2,64,2048]{2,0,1:T(2,128)(2,1)} %broadcast_select_fusion.4), channel_id=1, source_target_pairs={{0,8},{1,9},{2,10},{3,11},{4,12},{5,13},{6,14},{7,15},{8,0},{9,1},... | collective-permute-start | bytes 1572872 | tf_op jit(solution)/shard_map/ppermute | solution.py:15
  157.1 38.8 %collective-permute-start.4 = (bf16[2,64,2048]{2,0,1:T(2,128)(2,1)S(1)}, bf16[2,64,2048]{2,0,1:T(2,128)(2,1)S(1)}, u32[]{:S(2)}, u32[]{:S(2)}) collective-permute-start(bf16[2,64,2048]{2,0,1:T(2,128)(2,1)S(1)} %broadcast_select_fusion.3), channel_id=1, source_target_pairs={{0,16},{1,17},{2,18},{3,19},{4,20},{5,21},{6,22},{7,23},{8,24},{9,... | collective-permute-start | bytes 1572872 | tf_op jit(solution)/shard_map/ppermute | solution.py:15
  165.2 42.0 %collective-permute-start.10 = (bf16[2,64,2048]{2,0,1:T(2,128)(2,1)}, bf16[2,64,2048]{2,0,1:T(2,128)(2,1)S(1)}, u32[]{:S(2)}, u32[]{:S(2)}) collective-permute-start(bf16[2,64,2048]{2,0,1:T(2,128)(2,1)} %broadcast_select_fusion.2), channel_id=1, source_target_pairs={{0,16},{1,17},{2,18},{3,19},{4,20},{5,21},{6,22},{7,23},{8,24},{9,... | collective-permute-start | bytes 1572872 | tf_op jit(solution)/shard_map/ppermute | solution.py:15
  198.8 34.3 %collective-permute-start.5 = (bf16[2,64,2048]{2,0,1:T(2,128)(2,1)}, bf16[2,64,2048]{2,0,1:T(2,128)(2,1)S(1)}, u32[]{:S(2)}, u32[]{:S(2)}) collective-permute-start(bf16[2,64,2048]{2,0,1:T(2,128)(2,1)} %broadcast_select_fusion.1), channel_id=1, source_target_pairs={{0,32},{1,33},{2,34},{3,35},{4,36},{5,37},{6,38},{7,39},{8,40},{9,... | collective-permute-start | bytes 1572872 | tf_op jit(solution)/shard_map/ppermute | solution.py:15
  210.1 46.3 %collective-permute-start.11 = (bf16[2,64,2048]{2,0,1:T(2,128)(2,1)}, bf16[2,64,2048]{2,0,1:T(2,128)(2,1)S(1)}, u32[]{:S(2)}, u32[]{:S(2)}) collective-permute-start(bf16[2,64,2048]{2,0,1:T(2,128)(2,1)} %broadcast_select_fusion), channel_id=1, source_target_pairs={{0,32},{1,33},{2,34},{3,35},{4,36},{5,37},{6,38},{7,39},{8,40},{9,... | collective-permute-start | bytes 1572872 | tf_op jit(solution)/shard_map/ppermute | solution.py:15
  230.6 27.1 %copy-start.4 = (bf16[2,64,2048]{2,1,0:T(8,128)(2,1)S(1)}, bf16[2,64,2048]{2,1,0:T(8,128)(2,1)}, u32[]{:S(2)}) copy-start(bf16[2,64,2048]{2,1,0:T(8,128)(2,1)} %param.5) | copy-start | bytes 1572868
  263.0 2.0 copy-start.6
  265.1 3.2 copy-start.3
  266.1 8.7 %copy-start.2 = (bf16[2,16,448,128]{3,2,1,0:T(8,128)(2,1)S(1)}, bf16[2,16,448,128]{3,2,1,0:T(8,128)(2,1)}, u32[]{:S(2)}) copy-start(bf16[2,16,448,128]{3,2,1,0:T(8,128)(2,1)} %bitcast_dynamic-update-slice_fusion.5) | copy-start | bytes 11010052
  269.1 116.2 %collective-permute-start.18 = (bf16[2,16,64,128]{3,2,1,0:T(8,128)(2,1)}, bf16[2,16,64,128]{3,2,1,0:T(8,128)(2,1)}, u32[]{:S(2)}, u32[]{:S(2)}) collective-permute-start(bf16[2,16,64,128]{3,2,1,0:T(8,128)(2,1)} %slice.726), channel_id=1, source_target_pairs={{0,32},{1,33},{2,34},{3,35},{4,36},{5,37},{6,38},{7,39},{8,40},{9,... | collective-permute-start | bytes 1572872 | tf_op jit(solution)/shard_map/ppermute | solution.py:15
  377.3 9.7 %slice-start = ((s8[7340032]{0:T(1024)(128)(4,1)}), s8[4194304]{0:T(1024)(128)(4,1)S(1)}, s32[]{:S(2)}) async-start(s8[7340032]{0:T(1024)(128)(4,1)} %bitcast.564), calls=%async_computation | async-start | bytes 8388608
  378.2 8.7 %slice-start.1 = ((s8[7340032]{0:T(1024)(128)(4,1)}), s8[3145728]{0:T(1024)(128)(4,1)S(1)}, s32[]{:S(2)}) async-start(s8[7340032]{0:T(1024)(128)(4,1)} %bitcast.564), calls=%async_computation.1 | async-start | bytes 6291456
  379.5 30.2 %collective-permute-start.12 = (bf16[2,16,64,128]{3,2,1,0:T(8,128)(2,1)S(1)}, bf16[2,16,64,128]{3,2,1,0:T(8,128)(2,1)S(1)}, u32[]{:S(2)}, u32[]{:S(2)}) collective-permute-start(bf16[2,16,64,128]{3,2,1,0:T(8,128)(2,1)S(1)} %slice.727), channel_id=1, source_target_pairs={{0,32},{1,33},{2,34},{3,35},{4,36},{5,37},{6,38},{7,39},{8,40},{9,... | collective-permute-start | bytes 1572872 | tf_op jit(solution)/shard_map/ppermute | solution.py:15
  387.2 55.4 %collective-permute-start.19 = (bf16[2,16,64,128]{3,2,1,0:T(8,128)(2,1)S(1)}, bf16[2,16,64,128]{3,2,1,0:T(8,128)(2,1)S(1)}, u32[]{:S(2)}, u32[]{:S(2)}) collective-permute-start(bf16[2,16,64,128]{3,2,1,0:T(8,128)(2,1)S(1)} %fusion.17), channel_id=1, source_target_pairs={{0,16},{1,17},{2,18},{3,19},{4,20},{5,21},{6,22},{7,23},{8,24},{9,... | collective-permute-start | bytes 1572872 | tf_op jit(solution)/shard_map/ppermute | solution.py:15
  410.5 43.3 %collective-permute-start.13 = (bf16[2,16,64,128]{3,2,1,0:T(8,128)(2,1)S(1)}, bf16[2,16,64,128]{3,2,1,0:T(8,128)(2,1)S(1)}, u32[]{:S(2)}, u32[]{:S(2)}) collective-permute-start(bf16[2,16,64,128]{3,2,1,0:T(8,128)(2,1)S(1)} %fusion.23), channel_id=1, source_target_pairs={{0,16},{1,17},{2,18},{3,19},{4,20},{5,21},{6,22},{7,23},{8,24},{9,... | collective-permute-start | bytes 1572872 | tf_op jit(solution)/shard_map/ppermute | solution.py:15
  443.8 21.2 %collective-permute-start.20 = (bf16[2,16,64,128]{3,2,1,0:T(8,128)(2,1)S(1)}, bf16[2,16,64,128]{3,2,1,0:T(8,128)(2,1)S(1)}, u32[]{:S(2)}, u32[]{:S(2)}) collective-permute-start(bf16[2,16,64,128]{3,2,1,0:T(8,128)(2,1)S(1)} %fusion.16), channel_id=1, source_target_pairs={{0,8},{1,9},{2,10},{3,11},{4,12},{5,13},{6,14},{7,15},{8,0},{9,1},... | collective-permute-start | bytes 1572872 | tf_op jit(solution)/shard_map/ppermute | solution.py:15
  455.0 21.2 %collective-permute-start.14 = (bf16[2,16,64,128]{3,2,1,0:T(8,128)(2,1)S(1)}, bf16[2,16,64,128]{3,2,1,0:T(8,128)(2,1)S(1)}, u32[]{:S(2)}, u32[]{:S(2)}) collective-permute-start(bf16[2,16,64,128]{3,2,1,0:T(8,128)(2,1)S(1)} %fusion.22), channel_id=1, source_target_pairs={{0,8},{1,9},{2,10},{3,11},{4,12},{5,13},{6,14},{7,15},{8,0},{9,1},... | collective-permute-start | bytes 1572872 | tf_op jit(solution)/shard_map/ppermute | solution.py:15
  466.3 41.4 %collective-permute-start.21 = (bf16[2,16,64,128]{3,2,1,0:T(8,128)(2,1)S(1)}, bf16[2,16,64,128]{3,2,1,0:T(8,128)(2,1)S(1)}, u32[]{:S(2)}, u32[]{:S(2)}) collective-permute-start(bf16[2,16,64,128]{3,2,1,0:T(8,128)(2,1)S(1)} %fusion.15), channel_id=1, source_target_pairs={{0,4},{1,5},{2,6},{3,7},{4,0},{5,1},{6,2},{7,3},{8,12},{9,13},{10,... | collective-permute-start | bytes 1572872 | tf_op jit(solution)/shard_map/ppermute | solution.py:15
  477.5 41.5 %collective-permute-start.15 = (bf16[2,16,64,128]{3,2,1,0:T(8,128)(2,1)S(1)}, bf16[2,16,64,128]{3,2,1,0:T(8,128)(2,1)S(1)}, u32[]{:S(2)}, u32[]{:S(2)}) collective-permute-start(bf16[2,16,64,128]{3,2,1,0:T(8,128)(2,1)S(1)} %fusion.21), channel_id=1, source_target_pairs={{0,4},{1,5},{2,6},{3,7},{4,0},{5,1},{6,2},{7,3},{8,12},{9,13},{10,... | collective-permute-start | bytes 1572872 | tf_op jit(solution)/shard_map/ppermute | solution.py:15
  508.9 45.0 %collective-permute-start.22 = (bf16[2,16,64,128]{3,2,1,0:T(8,128)(2,1)S(1)}, bf16[2,16,64,128]{3,2,1,0:T(8,128)(2,1)S(1)}, u32[]{:S(2)}, u32[]{:S(2)}) collective-permute-start(bf16[2,16,64,128]{3,2,1,0:T(8,128)(2,1)S(1)} %fusion.14), channel_id=1, source_target_pairs={{0,2},{1,3},{2,0},{3,1},{4,6},{5,7},{6,4},{7,5},{8,10},{9,11},{10,... | collective-permute-start | bytes 1572872 | tf_op jit(solution)/shard_map/ppermute | solution.py:15
  520.2 44.9 %collective-permute-start.16 = (bf16[2,16,64,128]{3,2,1,0:T(8,128)(2,1)S(1)}, bf16[2,16,64,128]{3,2,1,0:T(8,128)(2,1)S(1)}, u32[]{:S(2)}, u32[]{:S(2)}) collective-permute-start(bf16[2,16,64,128]{3,2,1,0:T(8,128)(2,1)S(1)} %fusion.20), channel_id=1, source_target_pairs={{0,2},{1,3},{2,0},{3,1},{4,6},{5,7},{6,4},{7,5},{8,10},{9,11},{10,... | collective-permute-start | bytes 1572872 | tf_op jit(solution)/shard_map/ppermute | solution.py:15
  555.1 21.2 %collective-permute-start.23 = (bf16[2,16,64,128]{3,2,1,0:T(8,128)(2,1)S(1)}, bf16[2,16,64,128]{3,2,1,0:T(8,128)(2,1)S(1)}, u32[]{:S(2)}, u32[]{:S(2)}) collective-permute-start(bf16[2,16,64,128]{3,2,1,0:T(8,128)(2,1)S(1)} %fusion.13), channel_id=1, source_target_pairs={{0,1},{1,0},{2,3},{3,2},{4,5},{5,4},{6,7},{7,6},{8,9},{9,8},{10,11... | collective-permute-start | bytes 1572872 | tf_op jit(solution)/shard_map/ppermute | solution.py:15
  566.4 21.2 %collective-permute-start.17 = (bf16[2,16,64,128]{3,2,1,0:T(8,128)(2,1)S(1)}, bf16[2,16,64,128]{3,2,1,0:T(8,128)(2,1)S(1)}, u32[]{:S(2)}, u32[]{:S(2)}) collective-permute-start(bf16[2,16,64,128]{3,2,1,0:T(8,128)(2,1)S(1)} %fusion.19), channel_id=1, source_target_pairs={{0,1},{1,0},{2,3},{3,2},{4,5},{5,4},{6,7},{7,6},{8,9},{9,8},{10,11... | collective-permute-start | bytes 1572872 | tf_op jit(solution)/shard_map/ppermute | solution.py:15
  576.7 12.2 %copy-start.1 = (bf16[2,64,2048]{2,1,0:T(8,128)(2,1)S(1)}, bf16[2,64,2048]{2,1,0:T(8,128)(2,1)}, u32[]{:S(2)}) copy-start(bf16[2,64,2048]{2,1,0:T(8,128)(2,1)} %param.8) | copy-start | bytes 1572868
where the time goes:
time: 599 us; the launch traced here: 589 us
  waiting for transfers between devices  252 us (42%)
  starting transfers between devices  135 us (23%)
  blocking collectives  102 us (17%)
  other arithmetic  45 us (8%)
  local copies, waits for them, and re-layouts  42.2 us (7%)
  matrix products  10.8 us (2%)
    ppermute x24, waiting for transfers between devices, from_partner(): return lax.ppermute(value, axis, pairs)  252 us
    ppermute x24, starting transfers between devices, from_partner(): return lax.ppermute(value, axis, pairs)  135 us
    psum x1, blocking collectives, shards(): slope_grad = lax.psum(slope_part, ('dp', 'ctx'))  102 us
    unnamed x32, local copies, waits for them, and re-layouts  18.5 us
    select_n x10, other arithmetic, merge_level(): jnp.where(flag == 1, jnp.concatenate([other_small, own_small], axis=1), j...  15.5 us
  transfers between devices with their start and end apart: 24, of which 17 were waited for; matrix products, arithmetic and copies ran while one was open for 14% of the time, Pallas kernels for 0%

commit v1 on v0

--- a/solution.py
+++ b/solution.py
@@ -129,7 +129,7 @@
     query_part, key_part, value_part, slope_part = attend(
         query_four, key_set, value_set, grad_four, level_slope, block
     )
-    slope_grad = lax.psum(slope_part, ("dp", "ctx"))
+    slope_grad = lax.psum(lax.psum(slope_part, "ctx"), "dp")
     head = width // heads
     grad_keys = jnp.zeros((seqs, heads, block, head), jnp.float32)
     grad_values = jnp.zeros((seqs, heads, block, head), jnp.float32)

time: 599 us -> 635 us (1.060)
  waiting for transfers between devices: 252 us -> 189 us
  blocking collectives: 102 us -> 161 us
  starting transfers between devices: 135 us -> 169 us
    ppermute x24, waiting for transfers between devices: 252 us -> 189 us  [from_partner(): return lax.ppermute(value, axis, pairs)]
    psum x1 -> x2, blocking collectives: 102 us -> 161 us  [shards(): slope_grad = lax.psum(lax.psum(slope_part, 'ctx'), 'dp')]
    ppermute x24, starting transfers between devices: 135 us -> 169 us  [from_partner(): return lax.ppermute(value, axis, pairs)]
    unnamed x32 -> x36, local copies, waits for them, and re-layouts: 18.5 us -> 22.4 us
  transfers between devices with their start and end apart: 24 -> 24, of which waited for: 17 -> 15; matrix products, arithmetic and copies ran while one was open for 14% -> 13% of each run, Pallas kernels for 0% -> 0%
where the time goes in v1:
time: 635 us; the launch traced here: 625 us
  waiting for transfers between devices  189 us (30%)
  starting transfers between devices  169 us (27%)
  blocking collectives  161 us (25%)
  other arithmetic  47.3 us (7%)
  local copies, waits for them, and re-layouts  46 us (7%)
  matrix products  10.8 us (2%)
    ppermute x24, waiting for transfers between devices, from_partner(): return lax.ppermute(value, axis, pairs)  189 us
    ppermute x24, starting transfers between devices, from_partner(): return lax.ppermute(value, axis, pairs)  169 us
    psum x2, blocking collectives, shards(): slope_grad = lax.psum(lax.psum(slope_part, 'ctx'), 'dp')  161 us
    unnamed x36, local copies, waits for them, and re-layouts  22.4 us
    select_n x10, other arithmetic, merge_level(): jnp.where(flag == 1, jnp.concatenate([other_small, own_small], axis=1), j...  15.5 us
  transfers between devices with their start and end apart: 24, of which 15 were waited for; matrix products, arithmetic and copies ran while one was open for 13% of the time, Pallas kernels for 0%

profile of v1, /device:TPU:1, one launch (start us, length us, event | category | flops | bytes accessed | tf_op | source)
XLA Modules:
  0.0 625.3 jit_solution(18129209675489062471)
XLA Ops:
  0.7 5.0 collective-permute-start
  10.9 2.0 fusion.33
  15.2 9.6 %collective-permute-done.6 = bf16[2,64,2048]{2,1,0:T(8,128)(2,1)} collective-permute-done((bf16[2,64,2048]{2,1,0:T(8,128)(2,1)}, bf16[2,64,2048]{2,1,0:T(8,128)(2,1)}, u32[]{:S(2)}, u32[]{:S(2)}) %collective-permute-start.6) | collective-permute-done | bytes 524320 | tf_op jit(solution)/shard_map/ppermute | solution.py:15
  30.0 9.8 %collective-permute-start.1 = (bf16[2,64,2048]{2,0,1:T(2,128)(2,1)S(1)}, bf16[2,64,2048]{2,0,1:T(2,128)(2,1)S(1)}, u32[]{:S(2)}, u32[]{:S(2)}) collective-permute-start(bf16[2,64,2048]{2,0,1:T(2,128)(2,1)S(1)} %broadcast_select_fusion.9), channel_id=1, source_target_pairs={{0,2},{1,3},{2,0},{3,1},{4,6},{5,7},{6,4},{7,5},{8,10},{9,11},{10,... | collective-permute-start | bytes 1572872 | tf_op jit(solution)/shard_map/ppermute | solution.py:15
  44.0 2.0 fusion.32
  46.0 2.0 fusion.29
  48.0 25.8 %collective-permute-done.1 = bf16[2,64,2048]{2,0,1:T(2,128)(2,1)S(1)} collective-permute-done((bf16[2,64,2048]{2,0,1:T(2,128)(2,1)S(1)}, bf16[2,64,2048]{2,0,1:T(2,128)(2,1)S(1)}, u32[]{:S(2)}, u32[]{:S(2)}) %collective-permute-start.1) | collective-permute-done | bytes 524320 | tf_op jit(solution)/shard_map/ppermute | solution.py:15
  76.5 8.4 %collective-permute-start.2 = (bf16[2,64,2048]{2,0,1:T(2,128)(2,1)S(1)}, bf16[2,64,2048]{2,0,1:T(2,128)(2,1)S(1)}, u32[]{:S(2)}, u32[]{:S(2)}) collective-permute-start(bf16[2,64,2048]{2,0,1:T(2,128)(2,1)S(1)} %broadcast_select_fusion.7), channel_id=1, source_target_pairs={{0,4},{1,5},{2,6},{3,7},{4,0},{5,1},{6,2},{7,3},{8,12},{9,13},{10,... | collective-permute-start | bytes 1572872 | tf_op jit(solution)/shard_map/ppermute | solution.py:15
  87.3 1.9 broadcast_select_fusion.6
  89.3 30.1 %collective-permute-start.8 = (bf16[2,64,2048]{2,0,1:T(2,128)(2,1)}, bf16[2,64,2048]{2,0,1:T(2,128)(2,1)S(1)}, u32[]{:S(2)}, u32[]{:S(2)}) collective-permute-start(bf16[2,64,2048]{2,0,1:T(2,128)(2,1)} %broadcast_select_fusion.6), channel_id=1, source_target_pairs={{0,4},{1,5},{2,6},{3,7},{4,0},{5,1},{6,2},{7,3},{8,12},{9,13},{10,... | collective-permute-start | bytes 1572872 | tf_op jit(solution)/shard_map/ppermute | solution.py:15
  120.5 2.1 bitcast_dynamic-update-slice_fusion.9
  128.0 3.2 collective-permute-start.3
  132.2 9.6 %collective-permute-done.8 = bf16[2,64,2048]{2,0,1:T(2,128)(2,1)S(1)} collective-permute-done((bf16[2,64,2048]{2,0,1:T(2,128)(2,1)}, bf16[2,64,2048]{2,0,1:T(2,128)(2,1)S(1)}, u32[]{:S(2)}, u32[]{:S(2)}) %collective-permute-start.8) | collective-permute-done | bytes 524320 | tf_op jit(solution)/shard_map/ppermute | solution.py:15
  142.8 1.9 broadcast_select_fusion.4
  144.7 3.6 collective-permute-start.9
  149.4 2.1 bitcast_dynamic-update-slice_fusion.8
  157.0 4.2 collective-permute-start.4
  163.2 1.9 broadcast_select_fusion.2
  165.1 2.0 collective-permute-start.10
  168.2 2.1 bitcast_dynamic-update-slice_fusion.7
  173.7 22.0 %collective-permute-done.4 = bf16[2,64,2048]{2,0,1:T(2,128)(2,1)S(1)} collective-permute-done((bf16[2,64,2048]{2,0,1:T(2,128)(2,1)S(1)}, bf16[2,64,2048]{2,0,1:T(2,128)(2,1)S(1)}, u32[]{:S(2)}, u32[]{:S(2)}) %collective-permute-start.4) | collective-permute-done | bytes 524320 | tf_op jit(solution)/shard_map/ppermute | solution.py:15
  198.6 6.3 %collective-permute-start.5 = (bf16[2,64,2048]{2,0,1:T(2,128)(2,1)}, bf16[2,64,2048]{2,0,1:T(2,128)(2,1)S(1)}, u32[]{:S(2)}, u32[]{:S(2)}) collective-permute-start(bf16[2,64,2048]{2,0,1:T(2,128)(2,1)} %broadcast_select_fusion.1), channel_id=1, source_target_pairs={{0,32},{1,33},{2,34},{3,35},{4,36},{5,37},{6,38},{7,39},{8,40},{9,... | collective-permute-start | bytes 1572872 | tf_op jit(solution)/shard_map/ppermute | solution.py:15
  204.9 2.1 collective-permute-done.10
  209.9 20.2 %collective-permute-start.11 = (bf16[2,64,2048]{2,0,1:T(2,128)(2,1)}, bf16[2,64,2048]{2,0,1:T(2,128)(2,1)S(1)}, u32[]{:S(2)}, u32[]{:S(2)}) collective-permute-start(bf16[2,64,2048]{2,0,1:T(2,128)(2,1)} %broadcast_select_fusion), channel_id=1, source_target_pairs={{0,32},{1,33},{2,34},{3,35},{4,36},{5,37},{6,38},{7,39},{8,40},{9,... | collective-permute-start | bytes 1572872 | tf_op jit(solution)/shard_map/ppermute | solution.py:15
  234.3 22.0 %collective-permute-done.11 = bf16[2,64,2048]{2,0,1:T(2,128)(2,1)S(1)} collective-permute-done((bf16[2,64,2048]{2,0,1:T(2,128)(2,1)}, bf16[2,64,2048]{2,0,1:T(2,128)(2,1)S(1)}, u32[]{:S(2)}, u32[]{:S(2)}) %collective-permute-start.11) | collective-permute-done | bytes 524320 | tf_op jit(solution)/shard_map/ppermute | solution.py:15
  257.7 3.7 fusion.31
  266.1 2.1 multiply_reduce_fusion
  269.1 5.7 collective-permute-start.18
  275.7 119.6 %psum.14 = f32[16]{0:T(128)S(1)} all-reduce(f32[16]{0:T(128)S(1)} %get-tuple-element.26), channel_id=1, replica_groups=mesh['dp'=8,'ctx'=64] {'ctx'}, use_global_device_ids=true, to_apply=%region_4.5 | all-reduce | flops 16 | bytes 128 | tf_op jit(solution)/shard_map/psum | solution.py:132
  397.4 3.0 copy-done.2
  400.5 5.6 collective-permute-start.12
  406.1 40.9 %psum.15 = f32[16]{0:T(128)} all-reduce(f32[16]{0:T(128)S(1)} %psum.14), channel_id=1, replica_groups=mesh['dp'=8,'ctx'=64] {'dp'}, use_global_device_ids=true, to_apply=%region_5.6 | all-reduce | flops 16 | bytes 128 | tf_op jit(solution)/shard_map/psum | solution.py:132
  450.3 2.2 collective-permute-start.19
  453.3 4.3 collective-permute-start.13
  457.5 19.2 %collective-permute-done.19 = bf16[2,16,64,128]{3,2,1,0:T(8,128)(2,1)S(1)} collective-permute-done((bf16[2,16,64,128]{3,2,1,0:T(8,128)(2,1)S(1)}, bf16[2,16,64,128]{3,2,1,0:T(8,128)(2,1)S(1)}, u32[]{:S(2)}, u32[]{:S(2)}) %collective-permute-start.19) | collective-permute-done | bytes 524320 | tf_op jit(solution)/shard_map/ppermute | solution.py:15
  481.1 6.9 %collective-permute-done.13 = bf16[2,16,64,128]{3,2,1,0:T(8,128)(2,1)S(1)} collective-permute-done((bf16[2,16,64,128]{3,2,1,0:T(8,128)(2,1)S(1)}, bf16[2,16,64,128]{3,2,1,0:T(8,128)(2,1)S(1)}, u32[]{:S(2)}, u32[]{:S(2)}) %collective-permute-start.13) | collective-permute-done | bytes 524320 | tf_op jit(solution)/shard_map/ppermute | solution.py:15
  489.3 2.1 collective-permute-start.14
  491.3 7.9 %collective-permute-done.20 = bf16[2,16,64,128]{3,2,1,0:T(8,128)(2,1)S(1)} collective-permute-done((bf16[2,16,64,128]{3,2,1,0:T(8,128)(2,1)S(1)}, bf16[2,16,64,128]{3,2,1,0:T(8,128)(2,1)S(1)}, u32[]{:S(2)}, u32[]{:S(2)}) %collective-permute-start.20) | collective-permute-done | bytes 524320 | tf_op jit(solution)/shard_map/ppermute | solution.py:15
  501.3 6.9 %collective-permute-start.21 = (bf16[2,16,64,128]{3,2,1,0:T(8,128)(2,1)S(1)}, bf16[2,16,64,128]{3,2,1,0:T(8,128)(2,1)S(1)}, u32[]{:S(2)}, u32[]{:S(2)}) collective-permute-start(bf16[2,16,64,128]{3,2,1,0:T(8,128)(2,1)S(1)} %fusion.15), channel_id=1, source_target_pairs={{0,4},{1,5},{2,6},{3,7},{4,0},{5,1},{6,2},{7,3},{8,12},{9,13},{10,... | collective-permute-start | bytes 1572872 | tf_op jit(solution)/shard_map/ppermute | solution.py:15
  508.2 2.3 collective-permute-done.14
  511.6 6.9 %collective-permute-start.15 = (bf16[2,16,64,128]{3,2,1,0:T(8,128)(2,1)S(1)}, bf16[2,16,64,128]{3,2,1,0:T(8,128)(2,1)S(1)}, u32[]{:S(2)}, u32[]{:S(2)}) collective-permute-start(bf16[2,16,64,128]{3,2,1,0:T(8,128)(2,1)S(1)} %fusion.21), channel_id=1, source_target_pairs={{0,4},{1,5},{2,6},{3,7},{4,0},{5,1},{6,2},{7,3},{8,12},{9,13},{10,... | collective-permute-start | bytes 1572872 | tf_op jit(solution)/shard_map/ppermute | solution.py:15
  518.5 3.9 collective-permute-done.21
  523.6 23.0 %collective-permute-start.22 = (bf16[2,16,64,128]{3,2,1,0:T(8,128)(2,1)S(1)}, bf16[2,16,64,128]{3,2,1,0:T(8,128)(2,1)S(1)}, u32[]{:S(2)}, u32[]{:S(2)}) collective-permute-start(bf16[2,16,64,128]{3,2,1,0:T(8,128)(2,1)S(1)} %fusion.14), channel_id=1, source_target_pairs={{0,2},{1,3},{2,0},{3,1},{4,6},{5,7},{6,4},{7,5},{8,10},{9,11},{10,... | collective-permute-start | bytes 1572872 | tf_op jit(solution)/shard_map/ppermute | solution.py:15
  547.9 10.4 %collective-permute-start.16 = (bf16[2,16,64,128]{3,2,1,0:T(8,128)(2,1)S(1)}, bf16[2,16,64,128]{3,2,1,0:T(8,128)(2,1)S(1)}, u32[]{:S(2)}, u32[]{:S(2)}) collective-permute-start(bf16[2,16,64,128]{3,2,1,0:T(8,128)(2,1)S(1)} %fusion.20), channel_id=1, source_target_pairs={{0,2},{1,3},{2,0},{3,1},{4,6},{5,7},{6,4},{7,5},{8,10},{9,11},{10,... | collective-permute-start | bytes 1572872 | tf_op jit(solution)/shard_map/ppermute | solution.py:15
  558.3 31.6 %collective-permute-done.22 = bf16[2,16,64,128]{3,2,1,0:T(8,128)(2,1)S(1)} collective-permute-done((bf16[2,16,64,128]{3,2,1,0:T(8,128)(2,1)S(1)}, bf16[2,16,64,128]{3,2,1,0:T(8,128)(2,1)S(1)}, u32[]{:S(2)}, u32[]{:S(2)}) %collective-permute-start.22) | collective-permute-done | bytes 524320 | tf_op jit(solution)/shard_map/ppermute | solution.py:15
  593.0 8.2 %collective-permute-done.16 = bf16[2,16,64,128]{3,2,1,0:T(8,128)(2,1)S(1)} collective-permute-done((bf16[2,16,64,128]{3,2,1,0:T(8,128)(2,1)S(1)}, bf16[2,16,64,128]{3,2,1,0:T(8,128)(2,1)S(1)}, u32[]{:S(2)}, u32[]{:S(2)}) %collective-permute-start.16) | collective-permute-done | bytes 524320 | tf_op jit(solution)/shard_map/ppermute | solution.py:15
  604.3 8.1 %collective-permute-done.23 = bf16[2,16,64,128]{3,2,1,0:T(8,128)(2,1)S(1)} collective-permute-done((bf16[2,16,64,128]{3,2,1,0:T(8,128)(2,1)S(1)}, bf16[2,16,64,128]{3,2,1,0:T(8,128)(2,1)S(1)}, u32[]{:S(2)}, u32[]{:S(2)}) %collective-permute-start.23) | collective-permute-done | bytes 524320 | tf_op jit(solution)/shard_map/ppermute | solution.py:15
  613.6 9.9 %collective-permute-done.17 = bf16[2,16,64,128]{3,2,1,0:T(8,128)(2,1)S(1)} collective-permute-done((bf16[2,16,64,128]{3,2,1,0:T(8,128)(2,1)S(1)}, bf16[2,16,64,128]{3,2,1,0:T(8,128)(2,1)S(1)}, u32[]{:S(2)}, u32[]{:S(2)}) %collective-permute-start.17) | collective-permute-done | bytes 524320 | tf_op jit(solution)/shard_map/ppermute | solution.py:15
  (166 shorter events, 86.9 us)
Async XLA Ops:
  0.6 262.3 %copy-start = (bf16[2,64,2048]{2,1,0:T(8,128)(2,1)S(1)}, bf16[2,64,2048]{2,1,0:T(8,128)(2,1)}, u32[]{:S(2)}) copy-start(bf16[2,64,2048]{2,1,0:T(8,128)(2,1)} %param.8) | copy-start | bytes 1572868
  0.6 12.2 %copy-start.7 = (bf16[2,64,2048]{2,1,0:T(8,128)(2,1)S(1)}, bf16[2,64,2048]{2,1,0:T(8,128)(2,1)}, u32[]{:S(2)}) copy-start(bf16[2,64,2048]{2,1,0:T(8,128)(2,1)} %param.7) | copy-start | bytes 1572868
  0.7 26.2 %collective-permute-start = (bf16[2,64,2048]{2,1,0:T(8,128)(2,1)}, bf16[2,64,2048]{2,1,0:T(8,128)(2,1)}, u32[]{:S(2)}, u32[]{:S(2)}) collective-permute-start(bf16[2,64,2048]{2,1,0:T(8,128)(2,1)} %param.6), channel_id=1, source_target_pairs={{0,1},{1,0},{2,3},{3,2},{4,5},{5,4},{6,7},{7,6},{8,9},{9,8},{10,11... | collective-permute-start | bytes 1572872 | tf_op jit(solution)/shard_map/ppermute | solution.py:15
  5.6 19.1 %collective-permute-start.6 = (bf16[2,64,2048]{2,1,0:T(8,128)(2,1)}, bf16[2,64,2048]{2,1,0:T(8,128)(2,1)}, u32[]{:S(2)}, u32[]{:S(2)}) collective-permute-start(bf16[2,64,2048]{2,1,0:T(8,128)(2,1)} %param.7), channel_id=1, source_target_pairs={{0,1},{1,0},{2,3},{3,2},{4,5},{5,4},{6,7},{7,6},{8,9},{9,8},{10,11... | collective-permute-start | bytes 1572872 | tf_op jit(solution)/shard_map/ppermute | solution.py:15
  7.7 7.0 %copy-start.9 = (f32[16]{0:T(128)S(1)}, f32[16]{0:T(128)}, u32[]{:S(2)}) copy-start(f32[16]{0:T(128)} %param.9) | copy-start | bytes 196
  30.0 43.8 %collective-permute-start.1 = (bf16[2,64,2048]{2,0,1:T(2,128)(2,1)S(1)}, bf16[2,64,2048]{2,0,1:T(2,128)(2,1)S(1)}, u32[]{:S(2)}, u32[]{:S(2)}) collective-permute-start(bf16[2,64,2048]{2,0,1:T(2,128)(2,1)S(1)} %broadcast_select_fusion.9), channel_id=1, source_target_pairs={{0,2},{1,3},{2,0},{3,1},{4,6},{5,7},{6,4},{7,5},{8,10},{9,11},{10,... | collective-permute-start | bytes 1572872 | tf_op jit(solution)/shard_map/ppermute | solution.py:15
  41.5 44.3 %collective-permute-start.7 = (bf16[2,64,2048]{2,0,1:T(2,128)(2,1)S(1)}, bf16[2,64,2048]{2,0,1:T(2,128)(2,1)S(1)}, u32[]{:S(2)}, u32[]{:S(2)}) collective-permute-start(bf16[2,64,2048]{2,0,1:T(2,128)(2,1)S(1)} %broadcast_select_fusion.8), channel_id=1, source_target_pairs={{0,2},{1,3},{2,0},{3,1},{4,6},{5,7},{6,4},{7,5},{8,10},{9,11},{10,... | collective-permute-start | bytes 1572872 | tf_op jit(solution)/shard_map/ppermute | solution.py:15
  76.5 49.4 %collective-permute-start.2 = (bf16[2,64,2048]{2,0,1:T(2,128)(2,1)S(1)}, bf16[2,64,2048]{2,0,1:T(2,128)(2,1)S(1)}, u32[]{:S(2)}, u32[]{:S(2)}) collective-permute-start(bf16[2,64,2048]{2,0,1:T(2,128)(2,1)S(1)} %broadcast_select_fusion.7), channel_id=1, source_target_pairs={{0,4},{1,5},{2,6},{3,7},{4,0},{5,1},{6,2},{7,3},{8,12},{9,13},{10,... | collective-permute-start | bytes 1572872 | tf_op jit(solution)/shard_map/ppermute | solution.py:15
  89.3 52.5 %collective-permute-start.8 = (bf16[2,64,2048]{2,0,1:T(2,128)(2,1)}, bf16[2,64,2048]{2,0,1:T(2,128)(2,1)S(1)}, u32[]{:S(2)}, u32[]{:S(2)}) collective-permute-start(bf16[2,64,2048]{2,0,1:T(2,128)(2,1)} %broadcast_select_fusion.6), channel_id=1, source_target_pairs={{0,4},{1,5},{2,6},{3,7},{4,0},{5,1},{6,2},{7,3},{8,12},{9,13},{10,... | collective-permute-start | bytes 1572872 | tf_op jit(solution)/shard_map/ppermute | solution.py:15
  128.0 26.8 %collective-permute-start.3 = (bf16[2,64,2048]{2,0,1:T(2,128)(2,1)S(1)}, bf16[2,64,2048]{2,0,1:T(2,128)(2,1)S(1)}, u32[]{:S(2)}, u32[]{:S(2)}) collective-permute-start(bf16[2,64,2048]{2,0,1:T(2,128)(2,1)S(1)} %broadcast_select_fusion.5), channel_id=1, source_target_pairs={{0,8},{1,9},{2,10},{3,11},{4,12},{5,13},{6,14},{7,15},{8,0},{9,1},... | collective-permute-start | bytes 1572872 | tf_op jit(solution)/shard_map/ppermute | solution.py:15
  144.7 17.5 %collective-permute-start.9 = (bf16[2,64,2048]{2,0,1:T(2,128)(2,1)}, bf16[2,64,2048]{2,0,1:T(2,128)(2,1)S(1)}, u32[]{:S(2)}, u32[]{:S(2)}) collective-permute-start(bf16[2,64,2048]{2,0,1:T(2,128)(2,1)} %broadcast_select_fusion.4), channel_id=1, source_target_pairs={{0,8},{1,9},{2,10},{3,11},{4,12},{5,13},{6,14},{7,15},{8,0},{9,1},... | collective-permute-start | bytes 1572872 | tf_op jit(solution)/shard_map/ppermute | solution.py:15
  157.0 38.7 %collective-permute-start.4 = (bf16[2,64,2048]{2,0,1:T(2,128)(2,1)S(1)}, bf16[2,64,2048]{2,0,1:T(2,128)(2,1)S(1)}, u32[]{:S(2)}, u32[]{:S(2)}) collective-permute-start(bf16[2,64,2048]{2,0,1:T(2,128)(2,1)S(1)} %broadcast_select_fusion.3), channel_id=1, source_target_pairs={{0,16},{1,17},{2,18},{3,19},{4,20},{5,21},{6,22},{7,23},{8,24},{9,... | collective-permute-start | bytes 1572872 | tf_op jit(solution)/shard_map/ppermute | solution.py:15
  165.1 41.9 %collective-permute-start.10 = (bf16[2,64,2048]{2,0,1:T(2,128)(2,1)}, bf16[2,64,2048]{2,0,1:T(2,128)(2,1)S(1)}, u32[]{:S(2)}, u32[]{:S(2)}) collective-permute-start(bf16[2,64,2048]{2,0,1:T(2,128)(2,1)} %broadcast_select_fusion.2), channel_id=1, source_target_pairs={{0,16},{1,17},{2,18},{3,19},{4,20},{5,21},{6,22},{7,23},{8,24},{9,... | collective-permute-start | bytes 1572872 | tf_op jit(solution)/shard_map/ppermute | solution.py:15
  198.6 34.3 %collective-permute-start.5 = (bf16[2,64,2048]{2,0,1:T(2,128)(2,1)}, bf16[2,64,2048]{2,0,1:T(2,128)(2,1)S(1)}, u32[]{:S(2)}, u32[]{:S(2)}) collective-permute-start(bf16[2,64,2048]{2,0,1:T(2,128)(2,1)} %broadcast_select_fusion.1), channel_id=1, source_target_pairs={{0,32},{1,33},{2,34},{3,35},{4,36},{5,37},{6,38},{7,39},{8,40},{9,... | collective-permute-start | bytes 1572872 | tf_op jit(solution)/shard_map/ppermute | solution.py:15
  209.9 46.4 %collective-permute-start.11 = (bf16[2,64,2048]{2,0,1:T(2,128)(2,1)}, bf16[2,64,2048]{2,0,1:T(2,128)(2,1)S(1)}, u32[]{:S(2)}, u32[]{:S(2)}) collective-permute-start(bf16[2,64,2048]{2,0,1:T(2,128)(2,1)} %broadcast_select_fusion), channel_id=1, source_target_pairs={{0,32},{1,33},{2,34},{3,35},{4,36},{5,37},{6,38},{7,39},{8,40},{9,... | collective-permute-start | bytes 1572872 | tf_op jit(solution)/shard_map/ppermute | solution.py:15
  230.5 27.1 %copy-start.6 = (bf16[2,64,2048]{2,1,0:T(8,128)(2,1)S(1)}, bf16[2,64,2048]{2,1,0:T(8,128)(2,1)}, u32[]{:S(2)}) copy-start(bf16[2,64,2048]{2,1,0:T(8,128)(2,1)} %param.5) | copy-start | bytes 1572868
  263.0 2.0 copy-start.8
  265.0 3.2 copy-start.5
  266.1 8.7 %copy-start.4 = (bf16[2,16,448,128]{3,2,1,0:T(8,128)(2,1)S(1)}, bf16[2,16,448,128]{3,2,1,0:T(8,128)(2,1)}, u32[]{:S(2)}) copy-start(bf16[2,16,448,128]{3,2,1,0:T(8,128)(2,1)} %bitcast_dynamic-update-slice_fusion.5) | copy-start | bytes 11010052
  269.1 178.0 %collective-permute-start.18 = (bf16[2,16,64,128]{3,2,1,0:T(8,128)(2,1)}, bf16[2,16,64,128]{3,2,1,0:T(8,128)(2,1)}, u32[]{:S(2)}, u32[]{:S(2)}) collective-permute-start(bf16[2,16,64,128]{3,2,1,0:T(8,128)(2,1)} %slice.726), channel_id=1, source_target_pairs={{0,32},{1,33},{2,34},{3,35},{4,36},{5,37},{6,38},{7,39},{8,40},{9,... | collective-permute-start | bytes 1572872 | tf_op jit(solution)/shard_map/ppermute | solution.py:15
  397.4 3.0 copy-start.2
  400.5 52.0 %collective-permute-start.12 = (bf16[2,16,64,128]{3,2,1,0:T(8,128)(2,1)S(1)}, bf16[2,16,64,128]{3,2,1,0:T(8,128)(2,1)S(1)}, u32[]{:S(2)}, u32[]{:S(2)}) collective-permute-start(bf16[2,16,64,128]{3,2,1,0:T(8,128)(2,1)S(1)} %slice.727), channel_id=1, source_target_pairs={{0,32},{1,33},{2,34},{3,35},{4,36},{5,37},{6,38},{7,39},{8,40},{9,... | collective-permute-start | bytes 1572872 | tf_op jit(solution)/shard_map/ppermute | solution.py:15
  448.7 4.4 copy-start.3
  450.3 26.5 %collective-permute-start.19 = (bf16[2,16,64,128]{3,2,1,0:T(8,128)(2,1)S(1)}, bf16[2,16,64,128]{3,2,1,0:T(8,128)(2,1)S(1)}, u32[]{:S(2)}, u32[]{:S(2)}) collective-permute-start(bf16[2,16,64,128]{3,2,1,0:T(8,128)(2,1)S(1)} %fusion.17), channel_id=1, source_target_pairs={{0,16},{1,17},{2,18},{3,19},{4,20},{5,21},{6,22},{7,23},{8,24},{9,... | collective-permute-start | bytes 1572872 | tf_op jit(solution)/shard_map/ppermute | solution.py:15
  453.3 34.8 %collective-permute-start.13 = (bf16[2,16,64,128]{3,2,1,0:T(8,128)(2,1)S(1)}, bf16[2,16,64,128]{3,2,1,0:T(8,128)(2,1)S(1)}, u32[]{:S(2)}, u32[]{:S(2)}) collective-permute-start(bf16[2,16,64,128]{3,2,1,0:T(8,128)(2,1)S(1)} %fusion.23), channel_id=1, source_target_pairs={{0,16},{1,17},{2,18},{3,19},{4,20},{5,21},{6,22},{7,23},{8,24},{9,... | collective-permute-start | bytes 1572872 | tf_op jit(solution)/shard_map/ppermute | solution.py:15
  479.2 20.0 %collective-permute-start.20 = (bf16[2,16,64,128]{3,2,1,0:T(8,128)(2,1)S(1)}, bf16[2,16,64,128]{3,2,1,0:T(8,128)(2,1)S(1)}, u32[]{:S(2)}, u32[]{:S(2)}) collective-permute-start(bf16[2,16,64,128]{3,2,1,0:T(8,128)(2,1)S(1)} %fusion.16), channel_id=1, source_target_pairs={{0,8},{1,9},{2,10},{3,11},{4,12},{5,13},{6,14},{7,15},{8,0},{9,1},... | collective-permute-start | bytes 1572872 | tf_op jit(solution)/shard_map/ppermute | solution.py:15
  488.6 11.6 %slice-start = ((s8[7340032]{0:T(1024)(128)(4,1)}), s8[4194304]{0:T(1024)(128)(4,1)S(1)}, s32[]{:S(2)}) async-start(s8[7340032]{0:T(1024)(128)(4,1)} %bitcast.564), calls=%async_computation | async-start | bytes 8388608
  489.3 21.2 %collective-permute-start.14 = (bf16[2,16,64,128]{3,2,1,0:T(8,128)(2,1)S(1)}, bf16[2,16,64,128]{3,2,1,0:T(8,128)(2,1)S(1)}, u32[]{:S(2)}, u32[]{:S(2)}) collective-permute-start(bf16[2,16,64,128]{3,2,1,0:T(8,128)(2,1)S(1)} %fusion.22), channel_id=1, source_target_pairs={{0,8},{1,9},{2,10},{3,11},{4,12},{5,13},{6,14},{7,15},{8,0},{9,1},... | collective-permute-start | bytes 1572872 | tf_op jit(solution)/shard_map/ppermute | solution.py:15
  499.2 1.9 slice-start.1
  501.3 21.2 %collective-permute-start.21 = (bf16[2,16,64,128]{3,2,1,0:T(8,128)(2,1)S(1)}, bf16[2,16,64,128]{3,2,1,0:T(8,128)(2,1)S(1)}, u32[]{:S(2)}, u32[]{:S(2)}) collective-permute-start(bf16[2,16,64,128]{3,2,1,0:T(8,128)(2,1)S(1)} %fusion.15), channel_id=1, source_target_pairs={{0,4},{1,5},{2,6},{3,7},{4,0},{5,1},{6,2},{7,3},{8,12},{9,13},{10,... | collective-permute-start | bytes 1572872 | tf_op jit(solution)/shard_map/ppermute | solution.py:15
  511.6 35.1 %collective-permute-start.15 = (bf16[2,16,64,128]{3,2,1,0:T(8,128)(2,1)S(1)}, bf16[2,16,64,128]{3,2,1,0:T(8,128)(2,1)S(1)}, u32[]{:S(2)}, u32[]{:S(2)}) collective-permute-start(bf16[2,16,64,128]{3,2,1,0:T(8,128)(2,1)S(1)} %fusion.21), channel_id=1, source_target_pairs={{0,4},{1,5},{2,6},{3,7},{4,0},{5,1},{6,2},{7,3},{8,12},{9,13},{10,... | collective-permute-start | bytes 1572872 | tf_op jit(solution)/shard_map/ppermute | solution.py:15
  523.6 66.2 %collective-permute-start.22 = (bf16[2,16,64,128]{3,2,1,0:T(8,128)(2,1)S(1)}, bf16[2,16,64,128]{3,2,1,0:T(8,128)(2,1)S(1)}, u32[]{:S(2)}, u32[]{:S(2)}) collective-permute-start(bf16[2,16,64,128]{3,2,1,0:T(8,128)(2,1)S(1)} %fusion.14), channel_id=1, source_target_pairs={{0,2},{1,3},{2,0},{3,1},{4,6},{5,7},{6,4},{7,5},{8,10},{9,11},{10,... | collective-permute-start | bytes 1572872 | tf_op jit(solution)/shard_map/ppermute | solution.py:15
  547.9 53.3 %collective-permute-start.16 = (bf16[2,16,64,128]{3,2,1,0:T(8,128)(2,1)S(1)}, bf16[2,16,64,128]{3,2,1,0:T(8,128)(2,1)S(1)}, u32[]{:S(2)}, u32[]{:S(2)}) collective-permute-start(bf16[2,16,64,128]{3,2,1,0:T(8,128)(2,1)S(1)} %fusion.20), channel_id=1, source_target_pairs={{0,2},{1,3},{2,0},{3,1},{4,6},{5,7},{6,4},{7,5},{8,10},{9,11},{10,... | collective-permute-start | bytes 1572872 | tf_op jit(solution)/shard_map/ppermute | solution.py:15
  591.0 21.3 %collective-permute-start.23 = (bf16[2,16,64,128]{3,2,1,0:T(8,128)(2,1)S(1)}, bf16[2,16,64,128]{3,2,1,0:T(8,128)(2,1)S(1)}, u32[]{:S(2)}, u32[]{:S(2)}) collective-permute-start(bf16[2,16,64,128]{3,2,1,0:T(8,128)(2,1)S(1)} %fusion.13), channel_id=1, source_target_pairs={{0,1},{1,0},{2,3},{3,2},{4,5},{5,4},{6,7},{7,6},{8,9},{9,8},{10,11... | collective-permute-start | bytes 1572872 | tf_op jit(solution)/shard_map/ppermute | solution.py:15
  602.3 21.2 %collective-permute-start.17 = (bf16[2,16,64,128]{3,2,1,0:T(8,128)(2,1)S(1)}, bf16[2,16,64,128]{3,2,1,0:T(8,128)(2,1)S(1)}, u32[]{:S(2)}, u32[]{:S(2)}) collective-permute-start(bf16[2,16,64,128]{3,2,1,0:T(8,128)(2,1)S(1)} %fusion.19), channel_id=1, source_target_pairs={{0,1},{1,0},{2,3},{3,2},{4,5},{5,4},{6,7},{7,6},{8,9},{9,8},{10,11... | collective-permute-start | bytes 1572872 | tf_op jit(solution)/shard_map/ppermute | solution.py:15
  612.7 12.2 %copy-start.1 = (bf16[2,64,2048]{2,1,0:T(8,128)(2,1)S(1)}, bf16[2,64,2048]{2,1,0:T(8,128)(2,1)}, u32[]{:S(2)}) copy-start(bf16[2,64,2048]{2,1,0:T(8,128)(2,1)} %param.8) | copy-start | bytes 1572868
